TPU v7x, 256 devices: a whole 4x4x8 slice. The times are simulated.
256 devices in a mesh: seq: 32 (over z, x_lo, core), dp: 8 (over y, x_hi).
Axes of the slice: x: 4 (x_hi: 2, x_lo: 2; x = x_hi * 2 + x_lo), y: 4, z: 8, core: 2. Of those that a mesh axis runs over, the one named last changes fastest.
Arguments:
- queries: bfloat16 [8, 4096, 2048], P('dp', 'seq'), may hold values from -18 to 18
- key_vectors: bfloat16 [8, 4096, 2048], P('dp', 'seq'), may hold values from -18 to 18
- value_vectors: bfloat16 [8, 4096, 2048], P('dp', 'seq'), may hold values from -6 to 6
- cotangent: bfloat16 [8, 4096, 2048], P('dp', 'seq'), may hold values from -6 to 6
- compress_kernel: bfloat16 [512, 128], replicated, may hold values from -0.25 to 0.25
- memory_reach: int32 [8, 32], P('dp', 'seq'), may hold values from 1 to 4, as said below
Outputs:
- attended: bfloat16 [8, 4096, 2048], P('dp', 'seq')
- grad_queries: bfloat16 [8, 4096, 2048], P('dp', 'seq')
- grad_keys: bfloat16 [8, 4096, 2048], P('dp', 'seq')
- grad_values: bfloat16 [8, 4096, 2048], P('dp', 'seq')
- grad_kernel: float32 [512, 128], P('seq')
Inputs may be any that keep to these rules, and one draw needn't show every extreme that they name: `memory_reach`: some segment reads 4 earlier segments and some reads 1.
All inputs are finite; a program needn't handle non-finite values.
Results may differ from a plain program's by a relative error of at most 0.0076.
Values may be sent and summed in bfloat16 or wider, within the bound.
A program may use at most 64 MiB of HBM per device.

v0:
```python
import jax
import jax.numpy as jnp
from jax import lax
from jax.sharding import PartitionSpec as P

H = 16
E = 128


def shifted(value, axis, steps):
    count = lax.axis_size(axis)
    initial, last = (max(0, -steps), min(count, count - steps))
    return lax.ppermute(value, axis, [(source, source + steps) for source in range(initial, last)])


def attend_block(query_rows, key_rows, value_rows, grad_rows, memory_keys, memory_values, visible):
    segment_len = query_rows.shape[0]
    slot_rows = segment_len // 4
    span_len = 2 * segment_len
    score_scale = E ** (-0.5)
    query_heads = query_rows.reshape(segment_len, H, E)
    grad_heads = grad_rows.reshape(segment_len, H, E)
    key_heads = jnp.concatenate([memory_keys, key_rows], 0).reshape(span_len, H, E)
    value_heads = jnp.concatenate([memory_values, value_rows], 0).reshape(span_len, H, E)
    columns = jnp.arange(span_len, dtype=jnp.int32)
    row_ids = jnp.arange(segment_len, dtype=jnp.int32)
    slot_of = jnp.minimum(columns // slot_rows, 3)
    memory_open = jnp.any(
        (slot_of[:, None] == jnp.arange(4, dtype=jnp.int32)[None, :]) & visible[None, :], axis=1
    )
    allowed = jnp.where(
        columns[None, :] < segment_len,
        memory_open[None, :],
        columns[None, :] - segment_len <= row_ids[:, None],
    )
    scores = (
        jnp.einsum("shd,lhd->hsl", query_heads, key_heads, preferred_element_type=jnp.float32)
        * score_scale
    )
    scores = jnp.where(allowed[None], scores, -1e30)
    highest = jnp.max(scores, axis=2, keepdims=True)
    raised = jnp.where(allowed[None], jnp.exp(scores - highest), 0.0)
    weights = raised / jnp.sum(raised, axis=2, keepdims=True)
    weights_low = weights.astype(jnp.bfloat16)
    attended = jnp.einsum(
        "hsl,lhd->shd", weights_low, value_heads, preferred_element_type=jnp.float32
    )
    grad_weights = jnp.einsum(
        "shd,lhd->hsl", grad_heads, value_heads, preferred_element_type=jnp.float32
    )
    row_delta = jnp.sum(weights * grad_weights, axis=2, keepdims=True)
    grad_scores = (weights * (grad_weights - row_delta) * score_scale).astype(jnp.bfloat16)
    grad_query = jnp.einsum(
        "hsl,lhd->shd", grad_scores, key_heads, preferred_element_type=jnp.float32
    )
    grad_key_list = jnp.einsum(
        "hsl,shd->lhd", grad_scores, query_heads, preferred_element_type=jnp.float32
    ).reshape(span_len, H * E)
    grad_value_list = jnp.einsum(
        "hsl,shd->lhd", weights_low, grad_heads, preferred_element_type=jnp.float32
    ).reshape(span_len, H * E)
    return (
        attended.reshape(segment_len, H * E).astype(jnp.bfloat16),
        grad_query.reshape(segment_len, H * E).astype(jnp.bfloat16),
        grad_key_list[segment_len:],
        grad_value_list[segment_len:],
        grad_key_list[:segment_len],
        grad_value_list[:segment_len],
    )


def local(queries, key_vectors, value_vectors, cotangent, compress_kernel, memory_reach):
    query_rows = queries[0]
    key_rows = key_vectors[0]
    value_rows = value_vectors[0]
    grad_rows = cotangent[0]
    segment_len = query_rows.shape[0]
    slot_rows = segment_len // 4
    kernel = compress_kernel.reshape(4, E, E)
    key_blocks = key_rows.reshape(slot_rows, 4, H, E)
    value_blocks = value_rows.reshape(slot_rows, 4, H, E)
    packed_keys = (
        jnp.einsum("mthe,tef->mhf", key_blocks, kernel, preferred_element_type=jnp.float32)
        .astype(jnp.bfloat16)
        .reshape(slot_rows, H * E)
    )
    packed_values = (
        jnp.einsum("mthe,tef->mhf", value_blocks, kernel, preferred_element_type=jnp.float32)
        .astype(jnp.bfloat16)
        .reshape(slot_rows, H * E)
    )
    received = []
    for offset in range(1, 5):
        received.append(shifted((packed_keys, packed_values), "seq", offset))
    memory_keys = jnp.concatenate([shifted_pair[0] for shifted_pair in received], 0)
    memory_values = jnp.concatenate([shifted_pair[1] for shifted_pair in received], 0)
    position = lax.axis_index("seq")
    slot_ids = jnp.arange(1, 5, dtype=jnp.int32)
    visible = (slot_ids <= memory_reach[0, 0]) & (position - slot_ids >= 0)
    attended, grad_query, local_keys, local_values, memory_grad_keys, memory_grad_values = (
        attend_block(
            query_rows, key_rows, value_rows, grad_rows, memory_keys, memory_values, visible
        )
    )
    slot_keys = memory_grad_keys.reshape(4, slot_rows, H * E)
    slot_values = memory_grad_values.reshape(4, slot_rows, H * E)
    summed_keys = jnp.zeros((slot_rows, H * E), jnp.float32)
    summed_values = jnp.zeros((slot_rows, H * E), jnp.float32)
    for offset in range(1, 5):
        arrived = shifted((slot_keys[offset - 1], slot_values[offset - 1]), "seq", -offset)
        summed_keys = summed_keys + arrived[0]
        summed_values = summed_values + arrived[1]
    packed_grad_keys = summed_keys.astype(jnp.bfloat16).reshape(slot_rows, H, E)
    packed_grad_values = summed_values.astype(jnp.bfloat16).reshape(slot_rows, H, E)
    back_keys = jnp.einsum(
        "mhf,tef->mthe", packed_grad_keys, kernel, preferred_element_type=jnp.float32
    ).reshape(segment_len, H * E)
    back_values = jnp.einsum(
        "mhf,tef->mthe", packed_grad_values, kernel, preferred_element_type=jnp.float32
    ).reshape(segment_len, H * E)
    key_grad = (local_keys + back_keys).astype(jnp.bfloat16)
    value_grad = (local_values + back_values).astype(jnp.bfloat16)
    kernel_terms = (
        jnp.einsum(
            "mthe,mhf->tef", key_blocks, packed_grad_keys, preferred_element_type=jnp.float32
        )
        + jnp.einsum(
            "mthe,mhf->tef", value_blocks, packed_grad_values, preferred_element_type=jnp.float32
        )
    ).reshape(4 * E, E)
    whole_sum = lax.psum(kernel_terms, ("seq", "dp"))
    share_rows = 4 * E // lax.axis_size("seq")
    grad_kernel = lax.dynamic_slice_in_dim(
        whole_sum, lax.axis_index("seq") * share_rows, share_rows, 0
    )
    return (attended[None], grad_query[None], key_grad[None], value_grad[None], grad_kernel)


def solution(mesh):
    return jax.shard_map(
        local,
        mesh=mesh,
        in_specs=(
            P("dp", "seq", None),
            P("dp", "seq", None),
            P("dp", "seq", None),
            P("dp", "seq", None),
            P(),
            P("dp", "seq"),
        ),
        out_specs=(
            P("dp", "seq", None),
            P("dp", "seq", None),
            P("dp", "seq", None),
            P("dp", "seq", None),
            P("seq", None),
        ),
        check_vma=False,
    )
```

profile of v0, /device:TPU:2, one launch (start us, length us, event | category | flops | bytes accessed | tf_op | source)
XLA Modules:
  0.0 406.7 jit_solution(10729442592492152735)
XLA Ops:
  9.5 3.8 collective-permute-start.3
  13.3 3.0 collective-permute-start.2
  16.2 3.4 collective-permute-start.1
  19.7 3.0 collective-permute-start
  23.8 2.8 collective-permute-start.4
  31.6 3.4 collective-permute-start.5
  35.9 3.9 collective-permute-done.5
  39.8 4.0 collective-permute-start.6
  43.8 3.7 collective-permute-done.6
  47.5 4.7 %collective-permute-start.7 = (bf16[32,2048]{1,0:T(8,128)(2,1)}, bf16[32,2048]{1,0:T(8,128)(2,1)S(1)}, u32[]{:S(2)}, u32[]{:S(2)}) collective-permute-start(bf16[32,2048]{1,0:T(8,128)(2,1)} %bitcast.201), channel_id=1, source_target_pairs={{0,32},{8,40},{16,48},{24,56},{32,64},{40,72},{48,80},{56,88},{64,... | collective-permute-start | bytes 393224 | tf_op jit(solution)/shard_map/ppermute | solution.py:13
  52.3 2.8 collective-permute-done.7
  61.5 2.8 concatenate.33
  64.3 2.9 fusion.18
  67.2 3.5 fusion.45
  70.7 3.0 convolution_convert_fusion.1
  74.2 6.5 %convolution_bitcast_fusion.1 = f32[256,16,128]{2,0,1:T(8,128)} fusion(f32[16,256,128]{2,1,0:T(8,128)} %fusion.18, bf16[128,16,128]{2,1,0:T(8,128)(2,1)} %bitcast.229, f32[16,128,256]{1,2,0:T(8,128)} %get-tuple-element.29, f32[16,128]{1,0:T(8,128)S(1)} %get-tuple-element.28), kind=kOutput, calls=%fused_computation.11 | convolution fusion | flops 137890048 | bytes 6823936 | tf_op jit(solution)/shard_map/hsl,shd->lhd/dot_general | solution.py:56
  90.1 5.6 %convolution_convert_fusion = bf16[16,128,128]{2,1,0:T(8,128)(2,1)} fusion(bf16[256,16,128]{2,0,1:T(8,128)(2,1)} %constant_dynamic-update-slice_fusion, f32[16,256,128]{2,1,0:T(8,128)} %fusion.18, f32[16,128,256]{1,2,0:T(8,128)} %get-tuple-element.29, f32[16,128]{1,0:T(8,128)S(1)} %get-tuple-element.28), kind=kOutput, calls=%fused_computation.14 | convolution fusion | flops 138152192 | bytes 5775360 | tf_op jit(solution)/shard_map/hsl,lhd->shd/dot_general | solution.py:53
  95.6 2.1 copy.102
  118.1 2.5 copy.99
  121.0 2.6 collective-permute-done.10
  123.6 3.7 collective-permute-done.11
  127.3 8.5 %collective-permute-done.9 = f32[32,2048]{1,0:T(8,128)} collective-permute-done((f32[32,2048]{1,0:T(8,128)}, f32[32,2048]{1,0:T(8,128)}, u32[]{:S(2)}, u32[]{:S(2)}) %collective-permute-start.9) | collective-permute-done | bytes 262176 | tf_op jit(solution)/shard_map/ppermute | solution.py:13
  139.6 2.7 copy.92
  146.8 251.8 %all-reduce.2.cloned.1.call-done = f32[512,128]{1,0:T(8,128)} async-done(((f32[512,128]{1,0:T(8,128)}), f32[512,128]{1,0:T(8,128)}) %all-reduce.2.cloned.1.call-update) | async-done | bytes 262160 | tf_op jit(solution)/shard_map/psum | solution.py:131
  (111 shorter events, 55.0 us)
Async XLA Ops:
  7.2 15.5 %copy-start.8 = (bf16[1,128,2048]{2,1,0:T(8,128)(2,1)S(1)}, bf16[1,128,2048]{2,1,0:T(8,128)(2,1)}, u32[]{:S(2)}) copy-start(bf16[1,128,2048]{2,1,0:T(8,128)(2,1)} %param.7) | copy-start | bytes 1572868
  7.2 391.3 %all-reduce.2.cloned.1.call-start = ((), (), s32[]{:S(2)}) async-start(), calls=%async_computation | async-start | bytes 524288 | tf_op jit(solution)/shard_map/psum | solution.py:131
  8.5 18.5 %copy-start.9 = (bf16[1,128,2048]{2,1,0:T(8,128)(2,1)S(1)}, bf16[1,128,2048]{2,1,0:T(8,128)(2,1)}, u32[]{:S(2)}) copy-start(bf16[1,128,2048]{2,1,0:T(8,128)(2,1)} %param.8) | copy-start | bytes 1572868
  9.5 51.0 %collective-permute-start.3 = (bf16[32,2048]{1,0:T(8,128)(2,1)}, bf16[32,2048]{1,0:T(8,128)(2,1)S(1)}, u32[]{:S(2)}, u32[]{:S(2)}) collective-permute-start(bf16[32,2048]{1,0:T(8,128)(2,1)} %bitcast.202), channel_id=1, source_target_pairs={{0,32},{8,40},{16,48},{24,56},{32,64},{40,72},{48,80},{56,88},{64,... | collective-permute-start | bytes 393224 | tf_op jit(solution)/shard_map/ppermute | solution.py:13
  13.3 45.3 %collective-permute-start.2 = (bf16[32,2048]{1,0:T(8,128)(2,1)}, bf16[32,2048]{1,0:T(8,128)(2,1)S(1)}, u32[]{:S(2)}, u32[]{:S(2)}) collective-permute-start(bf16[32,2048]{1,0:T(8,128)(2,1)} %bitcast.202), channel_id=1, source_target_pairs={{0,24},{8,32},{16,40},{24,48},{32,56},{40,64},{48,72},{56,80},{64,... | collective-permute-start | bytes 393224 | tf_op jit(solution)/shard_map/ppermute | solution.py:13
  16.2 41.1 %collective-permute-start.1 = (bf16[32,2048]{1,0:T(8,128)(2,1)}, bf16[32,2048]{1,0:T(8,128)(2,1)}, u32[]{:S(2)}, u32[]{:S(2)}) collective-permute-start(bf16[32,2048]{1,0:T(8,128)(2,1)} %bitcast.202), channel_id=1, source_target_pairs={{0,16},{8,24},{16,32},{24,40},{32,48},{40,56},{48,64},{56,72},{64,... | collective-permute-start | bytes 393224 | tf_op jit(solution)/shard_map/ppermute | solution.py:13
  19.7 36.5 %collective-permute-start = (bf16[32,2048]{1,0:T(8,128)(2,1)}, bf16[32,2048]{1,0:T(8,128)(2,1)}, u32[]{:S(2)}, u32[]{:S(2)}) collective-permute-start(bf16[32,2048]{1,0:T(8,128)(2,1)} %bitcast.202), channel_id=1, source_target_pairs={{0,8},{8,16},{16,24},{24,32},{32,40},{40,48},{48,56},{56,64},{64,7... | collective-permute-start | bytes 393224 | tf_op jit(solution)/shard_map/ppermute | solution.py:13
  22.7 5.9 %copy-start.10 = (bf16[1,128,2048]{2,1,0:T(8,128)(2,1)S(1)}, bf16[1,128,2048]{2,1,0:T(8,128)(2,1)}, u32[]{:S(2)}) copy-start(bf16[1,128,2048]{2,1,0:T(8,128)(2,1)} %param.6) | copy-start | bytes 1572868
  23.8 7.8 %collective-permute-start.4 = (bf16[32,2048]{1,0:T(8,128)(2,1)}, bf16[32,2048]{1,0:T(8,128)(2,1)}, u32[]{:S(2)}, u32[]{:S(2)}) collective-permute-start(bf16[32,2048]{1,0:T(8,128)(2,1)} %bitcast.201), channel_id=1, source_target_pairs={{0,8},{8,16},{16,24},{24,32},{32,40},{40,48},{48,56},{56,64},{64,7... | collective-permute-start | bytes 393224 | tf_op jit(solution)/shard_map/ppermute | solution.py:13
  31.6 8.2 %collective-permute-start.5 = (bf16[32,2048]{1,0:T(8,128)(2,1)}, bf16[32,2048]{1,0:T(8,128)(2,1)S(1)}, u32[]{:S(2)}, u32[]{:S(2)}) collective-permute-start(bf16[32,2048]{1,0:T(8,128)(2,1)} %bitcast.201), channel_id=1, source_target_pairs={{0,16},{8,24},{16,32},{24,40},{32,48},{40,56},{48,64},{56,72},{64,... | collective-permute-start | bytes 393224 | tf_op jit(solution)/shard_map/ppermute | solution.py:13
  39.8 7.7 %collective-permute-start.6 = (bf16[32,2048]{1,0:T(8,128)(2,1)}, bf16[32,2048]{1,0:T(8,128)(2,1)S(1)}, u32[]{:S(2)}, u32[]{:S(2)}) collective-permute-start(bf16[32,2048]{1,0:T(8,128)(2,1)} %bitcast.201), channel_id=1, source_target_pairs={{0,24},{8,32},{16,40},{24,48},{32,56},{40,64},{48,72},{56,80},{64,... | collective-permute-start | bytes 393224 | tf_op jit(solution)/shard_map/ppermute | solution.py:13
  47.5 7.6 %collective-permute-start.7 = (bf16[32,2048]{1,0:T(8,128)(2,1)}, bf16[32,2048]{1,0:T(8,128)(2,1)S(1)}, u32[]{:S(2)}, u32[]{:S(2)}) collective-permute-start(bf16[32,2048]{1,0:T(8,128)(2,1)} %bitcast.201), channel_id=1, source_target_pairs={{0,32},{8,40},{16,48},{24,56},{32,64},{40,72},{48,80},{56,88},{64,... | collective-permute-start | bytes 393224 | tf_op jit(solution)/shard_map/ppermute | solution.py:13
  74.2 21.5 %copy-start.4 = (f32[256,16,128]{2,0,1:T(8,128)}, f32[256,16,128]{2,0,1:T(8,128)S(1)}, u32[]{:S(2)}) copy-start(f32[256,16,128]{2,0,1:T(8,128)S(1)} %convolution_bitcast_fusion) | copy-start | bytes 6291460
  83.6 27.0 %collective-permute-start.12 = (f32[32,2048]{1,0:T(8,128)}, f32[32,2048]{1,0:T(8,128)}, u32[]{:S(2)}, u32[]{:S(2)}) collective-permute-start(f32[32,2048]{1,0:T(8,128)} %bitcast.196), channel_id=1, source_target_pairs={{8,0},{16,8},{24,16},{32,24},{40,32},{48,40},{56,48},{64,56},{72,6... | collective-permute-start | bytes 786440 | tf_op jit(solution)/shard_map/ppermute | solution.py:13
  85.5 26.4 %collective-permute-start.14 = (f32[32,2048]{1,0:T(8,128)}, f32[32,2048]{1,0:T(8,128)}, u32[]{:S(2)}, u32[]{:S(2)}) collective-permute-start(f32[32,2048]{1,0:T(8,128)} %bitcast.194), channel_id=1, source_target_pairs={{24,0},{32,8},{40,16},{48,24},{56,32},{64,40},{72,48},{80,56},{88,... | collective-permute-start | bytes 786440 | tf_op jit(solution)/shard_map/ppermute | solution.py:13
  86.8 26.4 %collective-permute-start.15 = (f32[32,2048]{1,0:T(8,128)}, f32[32,2048]{1,0:T(8,128)}, u32[]{:S(2)}, u32[]{:S(2)}) collective-permute-start(f32[32,2048]{1,0:T(8,128)} %bitcast.193), channel_id=1, source_target_pairs={{32,0},{40,8},{48,16},{56,24},{64,32},{72,40},{80,48},{88,56},{96,... | collective-permute-start | bytes 786440 | tf_op jit(solution)/shard_map/ppermute | solution.py:13
  88.1 27.2 %collective-permute-start.13 = (f32[32,2048]{1,0:T(8,128)}, f32[32,2048]{1,0:T(8,128)}, u32[]{:S(2)}, u32[]{:S(2)}) collective-permute-start(f32[32,2048]{1,0:T(8,128)} %bitcast.195), channel_id=1, source_target_pairs={{16,0},{24,8},{32,16},{40,24},{48,32},{56,40},{64,48},{72,56},{80,... | collective-permute-start | bytes 786440 | tf_op jit(solution)/shard_map/ppermute | solution.py:13
  95.6 4.2 %slice-start.1 = ((f32[256,16,128]{2,0,1:T(8,128)}), f32[128,16,128]{2,0,1:T(8,128)S(1)}, s32[]{:S(2)}) async-start(f32[256,16,128]{2,0,1:T(8,128)} %copy-done.4), calls=%async_computation.2 | async-start | bytes 2097152 | tf_op jit(solution)/shard_map/slice | solution.py:66
  100.2 3.2 slice-start
  108.7 12.3 %collective-permute-start.8 = (f32[32,2048]{1,0:T(8,128)}, f32[32,2048]{1,0:T(8,128)}, u32[]{:S(2)}, u32[]{:S(2)}) collective-permute-start(f32[32,2048]{1,0:T(8,128)} %bitcast.200), channel_id=1, source_target_pairs={{8,0},{16,8},{24,16},{32,24},{40,32},{48,40},{56,48},{64,56},{72,6... | collective-permute-start | bytes 786440 | tf_op jit(solution)/shard_map/ppermute | solution.py:13
  110.6 13.0 %collective-permute-start.10 = (f32[32,2048]{1,0:T(8,128)}, f32[32,2048]{1,0:T(8,128)}, u32[]{:S(2)}, u32[]{:S(2)}) collective-permute-start(f32[32,2048]{1,0:T(8,128)} %bitcast.198), channel_id=1, source_target_pairs={{24,0},{32,8},{40,16},{48,24},{56,32},{64,40},{72,48},{80,56},{88,... | collective-permute-start | bytes 786440 | tf_op jit(solution)/shard_map/ppermute | solution.py:13
  112.0 15.3 %collective-permute-start.11 = (f32[32,2048]{1,0:T(8,128)}, f32[32,2048]{1,0:T(8,128)}, u32[]{:S(2)}, u32[]{:S(2)}) collective-permute-start(f32[32,2048]{1,0:T(8,128)} %bitcast.197), channel_id=1, source_target_pairs={{32,0},{40,8},{48,16},{56,24},{64,32},{72,40},{80,48},{88,56},{96,... | collective-permute-start | bytes 786440 | tf_op jit(solution)/shard_map/ppermute | solution.py:13
  113.3 22.5 %collective-permute-start.9 = (f32[32,2048]{1,0:T(8,128)}, f32[32,2048]{1,0:T(8,128)}, u32[]{:S(2)}, u32[]{:S(2)}) collective-permute-start(f32[32,2048]{1,0:T(8,128)} %bitcast.235), channel_id=1, source_target_pairs={{16,0},{24,8},{32,16},{40,24},{48,32},{56,40},{64,48},{72,56},{80,... | collective-permute-start | bytes 786440 | tf_op jit(solution)/shard_map/ppermute | solution.py:13
  139.6 3.6 copy-start.1
  (11 other events, 23.5 us)
Sparse Core Ops, SparseCore 0:
  138.6 259.9 all-reduce.1
where the time goes:
time: 408 us; the launch traced here: 407 us
  waiting for transfers between devices  277 us (68%)
  local copies, waits for them, and re-layouts  44.6 us (11%)
  starting transfers between devices  41.2 us (10%)
  matrix products  24.5 us (6%)
  between operations  15.2 us (4%)
  other arithmetic  4.38 us (1%)
    psum x1, waiting for transfers between devices, local(): whole_sum = lax.psum(kernel_terms, ('seq', 'dp'))  252 us
    ppermute x16, starting transfers between devices, shifted(): lax.ppermute(value, axis, [(source, source + steps) for source in range(i...  41.1 us
    ppermute x16, waiting for transfers between devices, shifted(): lax.ppermute(value, axis, [(source, source + steps) for source in range(i...  25.1 us
    unnamed x52, local copies, waits for them, and re-layouts  18.1 us
  transfers between devices with their start and end apart: 17, of which 7 were waited for; matrix products, arithmetic and copies ran while one was open for 10% of the time, Pallas kernels for 0%

commit v1 on v0

--- a/solution.py
+++ b/solution.py
@@ -128,7 +128,7 @@
             "mthe,mhf->tef", value_blocks, packed_grad_values, preferred_element_type=jnp.float32
         )
     ).reshape(4 * E, E)
-    whole_sum = lax.psum(kernel_terms, ("seq", "dp"))
+    whole_sum = lax.psum(lax.psum(kernel_terms, "seq"), "dp")
     share_rows = 4 * E // lax.axis_size("seq")
     grad_kernel = lax.dynamic_slice_in_dim(
         whole_sum, lax.axis_index("seq") * share_rows, share_rows, 0

time: 408 us -> 473 us (1.16)
  waiting for transfers between devices: 277 us -> 346 us
    psum x1 -> x2, waiting for transfers between devices: 252 us -> 321 us  [local(): whole_sum = lax.psum(lax.psum(kernel_terms, 'seq'), 'dp')]
    unnamed x52 -> x46, local copies, waits for them, and re-layouts: 18.1 us -> 15.5 us
  transfers between devices with their start and end apart: 17 -> 18, of which waited for: 7 -> 8; matrix products, arithmetic and copies ran while one was open for 10% -> 8% of each run, Pallas kernels for 0% -> 0%
where the time goes in v1:
time: 473 us; the launch traced here: 471 us
  waiting for transfers between devices  346 us (73%)
  starting transfers between devices  41 us (9%)
  local copies, waits for them, and re-layouts  40.1 us (8%)
  matrix products  24.5 us (5%)
  between operations  15.2 us (3%)
  other arithmetic  4.8 us (1%)
    psum x2, waiting for transfers between devices, local(): whole_sum = lax.psum(lax.psum(kernel_terms, 'seq'), 'dp')  321 us
    ppermute x16, starting transfers between devices, shifted(): lax.ppermute(value, axis, [(source, source + steps) for source in range(i...  40.9 us
    ppermute x16, waiting for transfers between devices, shifted(): lax.ppermute(value, axis, [(source, source + steps) for source in range(i...  25.3 us
    unnamed x46, local copies, waits for them, and re-layouts  15.5 us
  transfers between devices with their start and end apart: 18, of which 8 were waited for; matrix products, arithmetic and copies ran while one was open for 8% of the time, Pallas kernels for 0%

profile of v1, /device:TPU:2, one launch (start us, length us, event | category | flops | bytes accessed | tf_op | source)
XLA Modules:
  0.0 471.4 jit_solution(17341328246579317476)
XLA Ops:
  9.5 3.8 collective-permute-start.3
  13.3 3.0 collective-permute-start.2
  16.2 3.4 collective-permute-start.1
  19.6 3.0 collective-permute-start
  23.8 2.8 collective-permute-start.4
  31.6 3.4 collective-permute-start.5
  35.9 3.9 collective-permute-done.5
  39.8 4.0 collective-permute-start.6
  43.8 3.7 collective-permute-done.6
  47.5 4.7 %collective-permute-start.7 = (bf16[32,2048]{1,0:T(8,128)(2,1)}, bf16[32,2048]{1,0:T(8,128)(2,1)S(1)}, u32[]{:S(2)}, u32[]{:S(2)}) collective-permute-start(bf16[32,2048]{1,0:T(8,128)(2,1)} %bitcast.201), channel_id=1, source_target_pairs={{0,32},{8,40},{16,48},{24,56},{32,64},{40,72},{48,80},{56,88},{64,... | collective-permute-start | bytes 393224 | tf_op jit(solution)/shard_map/ppermute | solution.py:13
  52.3 2.8 collective-permute-done.7
  61.5 2.8 concatenate.33
  64.3 2.9 fusion.18
  67.2 3.5 fusion.45
  70.7 3.0 convolution_convert_fusion.1
  74.2 6.5 %convolution_bitcast_fusion.1 = f32[256,16,128]{2,0,1:T(8,128)} fusion(f32[16,256,128]{2,1,0:T(8,128)} %fusion.18, bf16[128,16,128]{2,1,0:T(8,128)(2,1)} %bitcast.229, f32[16,128,256]{1,2,0:T(8,128)} %get-tuple-element.29, f32[16,128]{1,0:T(8,128)S(1)} %get-tuple-element.28), kind=kOutput, calls=%fused_computation.11 | convolution fusion | flops 137890048 | bytes 6823936 | tf_op jit(solution)/shard_map/hsl,shd->lhd/dot_general | solution.py:56
  90.1 5.6 %convolution_convert_fusion = bf16[16,128,128]{2,1,0:T(8,128)(2,1)} fusion(bf16[256,16,128]{2,0,1:T(8,128)(2,1)} %constant_dynamic-update-slice_fusion, f32[16,256,128]{2,1,0:T(8,128)} %fusion.18, f32[16,128,256]{1,2,0:T(8,128)} %get-tuple-element.29, f32[16,128]{1,0:T(8,128)S(1)} %get-tuple-element.28), kind=kOutput, calls=%fused_computation.14 | convolution fusion | flops 138152192 | bytes 5775360 | tf_op jit(solution)/shard_map/hsl,lhd->shd/dot_general | solution.py:53
  95.6 2.1 copy.102
  118.2 2.5 copy.99
  121.1 2.8 collective-permute-done.10
  123.9 3.7 collective-permute-done.11
  127.6 8.5 %collective-permute-done.9 = f32[32,2048]{1,0:T(8,128)} collective-permute-done((f32[32,2048]{1,0:T(8,128)}, f32[32,2048]{1,0:T(8,128)}, u32[]{:S(2)}, u32[]{:S(2)}) %collective-permute-start.9) | collective-permute-done | bytes 262176 | tf_op jit(solution)/shard_map/ppermute | solution.py:13
  141.6 226.0 %all-reduce.3.cloned.1.call-done = f32[512,128]{1,0:T(8,128)} async-done(((f32[512,128]{1,0:T(8,128)}), f32[512,128]{1,0:T(8,128)}) %all-reduce.3.cloned.1.call-update) | async-done | bytes 262160 | tf_op jit(solution)/shard_map/psum | solution.py:131
  368.7 94.6 %all-reduce.5.cloned.1.call-done = f32[512,128]{1,0:T(8,128)} async-done(((f32[512,128]{1,0:T(8,128)}), f32[512,128]{1,0:T(8,128)}) %all-reduce.5.cloned.1.call-update) | async-done | bytes 262160 | tf_op jit(solution)/shard_map/psum | solution.py:131
  (107 shorter events, 53.4 us)
Async XLA Ops:
  7.2 15.5 %copy-start.5 = (bf16[1,128,2048]{2,1,0:T(8,128)(2,1)S(1)}, bf16[1,128,2048]{2,1,0:T(8,128)(2,1)}, u32[]{:S(2)}) copy-start(bf16[1,128,2048]{2,1,0:T(8,128)(2,1)} %param.7) | copy-start | bytes 1572868
  7.2 360.4 %all-reduce.3.cloned.1.call-start = ((), (), s32[]{:S(2)}) async-start(), calls=%async_computation | async-start | bytes 524288 | tf_op jit(solution)/shard_map/psum | solution.py:131
  8.5 18.5 %copy-start.6 = (bf16[1,128,2048]{2,1,0:T(8,128)(2,1)S(1)}, bf16[1,128,2048]{2,1,0:T(8,128)(2,1)}, u32[]{:S(2)}) copy-start(bf16[1,128,2048]{2,1,0:T(8,128)(2,1)} %param.8) | copy-start | bytes 1572868
  9.5 51.0 %collective-permute-start.3 = (bf16[32,2048]{1,0:T(8,128)(2,1)}, bf16[32,2048]{1,0:T(8,128)(2,1)S(1)}, u32[]{:S(2)}, u32[]{:S(2)}) collective-permute-start(bf16[32,2048]{1,0:T(8,128)(2,1)} %bitcast.202), channel_id=1, source_target_pairs={{0,32},{8,40},{16,48},{24,56},{32,64},{40,72},{48,80},{56,88},{64,... | collective-permute-start | bytes 393224 | tf_op jit(solution)/shard_map/ppermute | solution.py:13
  13.3 45.2 %collective-permute-start.2 = (bf16[32,2048]{1,0:T(8,128)(2,1)}, bf16[32,2048]{1,0:T(8,128)(2,1)S(1)}, u32[]{:S(2)}, u32[]{:S(2)}) collective-permute-start(bf16[32,2048]{1,0:T(8,128)(2,1)} %bitcast.202), channel_id=1, source_target_pairs={{0,24},{8,32},{16,40},{24,48},{32,56},{40,64},{48,72},{56,80},{64,... | collective-permute-start | bytes 393224 | tf_op jit(solution)/shard_map/ppermute | solution.py:13
  16.2 41.1 %collective-permute-start.1 = (bf16[32,2048]{1,0:T(8,128)(2,1)}, bf16[32,2048]{1,0:T(8,128)(2,1)}, u32[]{:S(2)}, u32[]{:S(2)}) collective-permute-start(bf16[32,2048]{1,0:T(8,128)(2,1)} %bitcast.202), channel_id=1, source_target_pairs={{0,16},{8,24},{16,32},{24,40},{32,48},{40,56},{48,64},{56,72},{64,... | collective-permute-start | bytes 393224 | tf_op jit(solution)/shard_map/ppermute | solution.py:13
  19.6 36.5 %collective-permute-start = (bf16[32,2048]{1,0:T(8,128)(2,1)}, bf16[32,2048]{1,0:T(8,128)(2,1)}, u32[]{:S(2)}, u32[]{:S(2)}) collective-permute-start(bf16[32,2048]{1,0:T(8,128)(2,1)} %bitcast.202), channel_id=1, source_target_pairs={{0,8},{8,16},{16,24},{24,32},{32,40},{40,48},{48,56},{56,64},{64,7... | collective-permute-start | bytes 393224 | tf_op jit(solution)/shard_map/ppermute | solution.py:13
  22.7 5.9 %copy-start.7 = (bf16[1,128,2048]{2,1,0:T(8,128)(2,1)S(1)}, bf16[1,128,2048]{2,1,0:T(8,128)(2,1)}, u32[]{:S(2)}) copy-start(bf16[1,128,2048]{2,1,0:T(8,128)(2,1)} %param.6) | copy-start | bytes 1572868
  23.8 7.8 %collective-permute-start.4 = (bf16[32,2048]{1,0:T(8,128)(2,1)}, bf16[32,2048]{1,0:T(8,128)(2,1)}, u32[]{:S(2)}, u32[]{:S(2)}) collective-permute-start(bf16[32,2048]{1,0:T(8,128)(2,1)} %bitcast.201), channel_id=1, source_target_pairs={{0,8},{8,16},{16,24},{24,32},{32,40},{40,48},{48,56},{56,64},{64,7... | collective-permute-start | bytes 393224 | tf_op jit(solution)/shard_map/ppermute | solution.py:13
  31.6 8.2 %collective-permute-start.5 = (bf16[32,2048]{1,0:T(8,128)(2,1)}, bf16[32,2048]{1,0:T(8,128)(2,1)S(1)}, u32[]{:S(2)}, u32[]{:S(2)}) collective-permute-start(bf16[32,2048]{1,0:T(8,128)(2,1)} %bitcast.201), channel_id=1, source_target_pairs={{0,16},{8,24},{16,32},{24,40},{32,48},{40,56},{48,64},{56,72},{64,... | collective-permute-start | bytes 393224 | tf_op jit(solution)/shard_map/ppermute | solution.py:13
  39.8 7.7 %collective-permute-start.6 = (bf16[32,2048]{1,0:T(8,128)(2,1)}, bf16[32,2048]{1,0:T(8,128)(2,1)S(1)}, u32[]{:S(2)}, u32[]{:S(2)}) collective-permute-start(bf16[32,2048]{1,0:T(8,128)(2,1)} %bitcast.201), channel_id=1, source_target_pairs={{0,24},{8,32},{16,40},{24,48},{32,56},{40,64},{48,72},{56,80},{64,... | collective-permute-start | bytes 393224 | tf_op jit(solution)/shard_map/ppermute | solution.py:13
  47.5 7.6 %collective-permute-start.7 = (bf16[32,2048]{1,0:T(8,128)(2,1)}, bf16[32,2048]{1,0:T(8,128)(2,1)S(1)}, u32[]{:S(2)}, u32[]{:S(2)}) collective-permute-start(bf16[32,2048]{1,0:T(8,128)(2,1)} %bitcast.201), channel_id=1, source_target_pairs={{0,32},{8,40},{16,48},{24,56},{32,64},{40,72},{48,80},{56,88},{64,... | collective-permute-start | bytes 393224 | tf_op jit(solution)/shard_map/ppermute | solution.py:13
  74.2 21.5 %copy-start.2 = (f32[256,16,128]{2,0,1:T(8,128)}, f32[256,16,128]{2,0,1:T(8,128)S(1)}, u32[]{:S(2)}) copy-start(f32[256,16,128]{2,0,1:T(8,128)S(1)} %convolution_bitcast_fusion) | copy-start | bytes 6291460
  83.6 27.3 %collective-permute-start.12 = (f32[32,2048]{1,0:T(8,128)}, f32[32,2048]{1,0:T(8,128)}, u32[]{:S(2)}, u32[]{:S(2)}) collective-permute-start(f32[32,2048]{1,0:T(8,128)} %bitcast.196), channel_id=1, source_target_pairs={{8,0},{16,8},{24,16},{32,24},{40,32},{48,40},{56,48},{64,56},{72,6... | collective-permute-start | bytes 786440 | tf_op jit(solution)/shard_map/ppermute | solution.py:13
  85.5 26.7 %collective-permute-start.14 = (f32[32,2048]{1,0:T(8,128)}, f32[32,2048]{1,0:T(8,128)}, u32[]{:S(2)}, u32[]{:S(2)}) collective-permute-start(f32[32,2048]{1,0:T(8,128)} %bitcast.194), channel_id=1, source_target_pairs={{24,0},{32,8},{40,16},{48,24},{56,32},{64,40},{72,48},{80,56},{88,... | collective-permute-start | bytes 786440 | tf_op jit(solution)/shard_map/ppermute | solution.py:13
  86.8 26.7 %collective-permute-start.15 = (f32[32,2048]{1,0:T(8,128)}, f32[32,2048]{1,0:T(8,128)}, u32[]{:S(2)}, u32[]{:S(2)}) collective-permute-start(f32[32,2048]{1,0:T(8,128)} %bitcast.193), channel_id=1, source_target_pairs={{32,0},{40,8},{48,16},{56,24},{64,32},{72,40},{80,48},{88,56},{96,... | collective-permute-start | bytes 786440 | tf_op jit(solution)/shard_map/ppermute | solution.py:13
  88.1 27.4 %collective-permute-start.13 = (f32[32,2048]{1,0:T(8,128)}, f32[32,2048]{1,0:T(8,128)}, u32[]{:S(2)}, u32[]{:S(2)}) collective-permute-start(f32[32,2048]{1,0:T(8,128)} %bitcast.195), channel_id=1, source_target_pairs={{16,0},{24,8},{32,16},{40,24},{48,32},{56,40},{64,48},{72,56},{80,... | collective-permute-start | bytes 786440 | tf_op jit(solution)/shard_map/ppermute | solution.py:13
  95.6 4.2 slice-start
  109.0 12.1 %collective-permute-start.8 = (f32[32,2048]{1,0:T(8,128)}, f32[32,2048]{1,0:T(8,128)}, u32[]{:S(2)}, u32[]{:S(2)}) collective-permute-start(f32[32,2048]{1,0:T(8,128)} %bitcast.200), channel_id=1, source_target_pairs={{8,0},{16,8},{24,16},{32,24},{40,32},{48,40},{56,48},{64,56},{72,6... | collective-permute-start | bytes 786440 | tf_op jit(solution)/shard_map/ppermute | solution.py:13
  111.0 13.0 %collective-permute-start.10 = (f32[32,2048]{1,0:T(8,128)}, f32[32,2048]{1,0:T(8,128)}, u32[]{:S(2)}, u32[]{:S(2)}) collective-permute-start(f32[32,2048]{1,0:T(8,128)} %bitcast.198), channel_id=1, source_target_pairs={{24,0},{32,8},{40,16},{48,24},{56,32},{64,40},{72,48},{80,56},{88,... | collective-permute-start | bytes 786440 | tf_op jit(solution)/shard_map/ppermute | solution.py:13
  112.3 15.3 %collective-permute-start.11 = (f32[32,2048]{1,0:T(8,128)}, f32[32,2048]{1,0:T(8,128)}, u32[]{:S(2)}, u32[]{:S(2)}) collective-permute-start(f32[32,2048]{1,0:T(8,128)} %bitcast.197), channel_id=1, source_target_pairs={{32,0},{40,8},{48,16},{56,24},{64,32},{72,40},{80,48},{88,56},{96,... | collective-permute-start | bytes 786440 | tf_op jit(solution)/shard_map/ppermute | solution.py:13
  113.6 22.5 %collective-permute-start.9 = (f32[32,2048]{1,0:T(8,128)}, f32[32,2048]{1,0:T(8,128)}, u32[]{:S(2)}, u32[]{:S(2)}) collective-permute-start(f32[32,2048]{1,0:T(8,128)} %bitcast.235), channel_id=1, source_target_pairs={{16,0},{24,8},{32,16},{40,24},{48,32},{56,40},{64,48},{72,56},{80,... | collective-permute-start | bytes 786440 | tf_op jit(solution)/shard_map/ppermute | solution.py:13
  120.8 17.7 %copy-start.1 = (f32[128,16,128]{0,2,1:T(8,128)S(1)}, f32[128,16,128]{0,2,1:T(8,128)}, u32[]{:S(2)}) copy-start(f32[128,16,128]{0,2,1:T(8,128)} %copy.94) | copy-start | bytes 3145732
  138.4 324.9 %all-reduce.5.cloned.1.call-start = ((), (), s32[]{:S(2)}) async-start(), calls=%async_computation.1 | async-start | bytes 524288 | tf_op jit(solution)/shard_map/psum | solution.py:131
  (8 other events, 18.7 us)
Sparse Core Ops, SparseCore 0:
  138.5 228.9 all-reduce.2
  370.2 93.0 all-reduce.4
